TPU v7x, 512 devices: a whole 4x4x16 slice. The times are simulated.
512 devices in a mesh: gx: 8 (over y, core), yz: 64 (over x, z).
Axes of the slice: x: 4, y: 4, z: 16, core: 2. Of those that a mesh axis runs over, the one named last changes fastest.
Arguments:
- elem_tiles: bfloat16 [8192, 36864], P(('gx', 'yz')), may hold values from -0.0390625 to 0.0390625
- inv_factor: bfloat16 [1024, 36864], P(('gx', 'yz'))
- rhs: bfloat16 [1024, 192, 128], P(('gx', 'yz')), may hold values from -6 to 6
- mig_source: int32 [8, 128], P('gx'), may hold values from 0 to 127, as said below
- tile_target: int32 [8, 1024], P('gx'), may hold values from 0 to 1023, as said below
- col_index: int32 [1024, 8], P(('gx', 'yz')), may hold values from 0 to 5
Outputs:
- iterate: float32 [1024, 192, 128], P(('gx', 'yz'))
Inputs may be any that keep to these rules, and one draw needn't show every extreme that they name: `mig_source`: each slab's row is a permutation. A block moves only between owners whose indices differ in the highest bit (index and index + 32) or in the lowest bit (index and index xor 1), at most one block from a device for each of these two bits; every draw moves a block between owners 0 and 32 of each slab. `tile_target`: each slab's row is a permutation. Element tile t of owner a goes to owner (a + s_t) mod 64, with shifts s_t common to a slab's owners, one of them 64/2; at most 1 tiles go from one owner to one owner, and that many do from every owner.
All inputs are finite; a program needn't handle non-finite values.
Results may differ from a plain program's by a relative error of at most 0.0033.
Values may be sent and summed in bfloat16 or wider, within the bound.
A program may use at most 128 MiB of HBM per device.

v0:
```python
import jax
import jax.numpy as jnp
from jax import lax
from jax.sharding import PartitionSpec as P

HB = 2
ITERS = 3


def with_halo(cells, sides, width):
    for axis, dim in sides:
        count = lax.axis_size(axis)
        ends = count - 1
        head = lax.slice_in_dim(cells, 0, width, axis=dim)
        tail = lax.slice_in_dim(cells, cells.shape[dim] - width, cells.shape[dim], axis=dim)
        cells = jnp.concatenate(
            [
                lax.ppermute(tail, axis, [(i, (i + 1) % count) for i in range(ends)]),
                cells,
                lax.ppermute(head, axis, [((i + 1) % count, i) for i in range(ends)]),
            ],
            axis=dim,
        )
    return cells


def shards(elem_tiles, inv_factor, rhs, mig_source, tile_target, col_index):
    owners = lax.axis_size("yz")
    my_index = lax.axis_index("yz")
    tile_count = elem_tiles.shape[0]
    row_blocks = inv_factor.shape[0]
    block_order = rhs.shape[1]
    couplings = col_index.shape[1]
    slot_cap = (tile_count + owners - 1) // owners
    tile_map = tile_target[0]
    move_map = mig_source[0]
    all_dest = (tile_map // tile_count).reshape(owners, tile_count)
    earlier = jnp.arange(tile_count)[:, None] > jnp.arange(tile_count)[None, :]
    same_dest = all_dest[:, :, None] == all_dest[:, None, :]
    all_rank = jnp.sum(same_dest & earlier[None], axis=2)
    my_dest = all_dest[my_index]
    my_rank = all_rank[my_index]
    outgoing = jnp.zeros((owners * slot_cap, elem_tiles.shape[1]), jnp.bfloat16)
    outgoing = (
        outgoing.at[my_dest * slot_cap + my_rank].set(elem_tiles).reshape(owners, slot_cap, -1)
    )
    arrived = lax.all_to_all(outgoing, "yz", split_axis=0, concat_axis=0, tiled=True)
    wanted = my_index * tile_count + jnp.arange(tile_count, dtype=jnp.int32)
    matches = tile_map[None, :] == wanted[:, None]
    source_tile = jnp.sum(
        jnp.where(matches, jnp.arange(tile_map.shape[0], dtype=jnp.int32)[None, :], 0), axis=1
    )
    flat_rank = all_rank.reshape(-1)
    row_tiles = arrived.reshape(owners * slot_cap, -1)[
        source_tile // tile_count * slot_cap + flat_rank[source_tile]
    ]
    new_source = lax.dynamic_slice_in_dim(move_map, my_index * row_blocks, row_blocks)
    from_owner = new_source // row_blocks
    stays_home = from_owner == my_index
    own_blocks = inv_factor[new_source % row_blocks]
    by_owner = move_map.reshape(owners, row_blocks)
    leaving = (by_owner // row_blocks == my_index) & (jnp.arange(owners)[:, None] != my_index)
    local_slot = jnp.sum(jnp.where(leaving, by_owner % row_blocks, 0), axis=1)
    payload = jnp.where(
        jnp.any(leaving, axis=1)[:, None], inv_factor[local_slot], jnp.zeros((), jnp.bfloat16)
    )
    received = lax.all_to_all(payload[:, None, :], "yz", split_axis=0, concat_axis=0, tiled=True)
    factors = jnp.where(stays_home[:, None], own_blocks, received[from_owner, 0])
    factor_blocks = factors.reshape(row_blocks, block_order, block_order)
    tile_blocks = row_tiles.reshape(row_blocks, couplings, block_order, block_order)

    def precondition(vectors):
        return jnp.einsum(
            "rij,rjn->rin", factor_blocks, vectors, preferred_element_type=jnp.float32
        )

    iterate = precondition(rhs)
    for sweep_index in range(ITERS):
        rounded = iterate.astype(jnp.bfloat16)
        padded = with_halo(rounded, (("gx", 0),), HB)
        picked = padded[col_index]
        coupled = jnp.einsum(
            "rkij,rkjn->rin", tile_blocks, picked, preferred_element_type=jnp.float32
        )
        residual = (rhs.astype(jnp.float32) - (rounded.astype(jnp.float32) + coupled)).astype(
            jnp.bfloat16
        )
        iterate = iterate + precondition(residual)
    return iterate


def solution(mesh):
    placed = (
        P(("gx", "yz"), None),
        P(("gx", "yz"), None),
        P(("gx", "yz"), None, None),
        P("gx", None),
        P("gx", None),
        P(("gx", "yz"), None),
    )
    return jax.shard_map(
        shards, mesh=mesh, in_specs=placed, out_specs=P(("gx", "yz"), None, None), check_vma=False
    )
```

profile of v0, /device:TPU:1, one launch (start us, length us, event | category | flops | bytes accessed | tf_op | source)
XLA Modules:
  0.0 538.4 jit_solution(14977322753482297362)
XLA Ops:
  0.0 0.0 copy-start
  0.0 0.5 broadcast.557
  0.5 1.3 reduce.8
  1.8 0.1 reshape_squeeze.3
  2.0 0.2 fusion.34
  2.2 0.1 fusion.19
  2.3 0.0 copy-done
  2.3 5.7 %gather_fusion.1 = bf16[64,36864]{1,0:T(8,128)(2,1)} fusion(bf16[2,36864]{1,0:T(2,128)(2,1)S(1)} %copy-done, s32[1024]{0:T(1024)S(1)} %pad_clamp_fusion.3), kind=kCustom, calls=%fused_computation.1 | custom fusion | bytes 9437440 | tf_op jit(solution)/shard_map/gather | solution.py:65
  8.1 4.8 bitcast_select_fusion
  12.9 0.5 broadcast.561
  13.4 7.3 %reduce.10 = bf16[64,36864]{1,0:T(8,128)(2,1)} reduce(bf16[64,1,36864]{2,0,1:T(8,128)(2,1)} %bitcast_select_fusion, bf16[]{:T(256)} %broadcast.561), dimensions={1}, to_apply=%copy.21.reduce_sub_computation | reduce | bytes 9437186 | tf_op jit(solution)/shard_map/jit(_where)/select_n | solution.py:64
  20.8 8.2 %reshape.480 = bf16[64,2,18432]{2,1,0:T(2,128)(2,1)} reshape(bf16[64,36864]{1,0:T(8,128)(2,1)} %reduce.10) | data formatting | bytes 9437184
  29.0 19.5 %all-to-all-start = ((bf16[64,2,18432]{2,1,0:T(2,128)(2,1)}), bf16[64,2,18432]{2,1,0:T(2,128)(2,1)}, u32[]{:S(2)}, u32[]{:S(2)}) async-start(bf16[64,2,18432]{2,1,0:T(2,128)(2,1)} %reshape.480), calls=%async_computation | async-start | bytes 9437184 | tf_op jit(solution)/shard_map/all_to_all | solution.py:67
  48.5 0.0 copy-done.2
  48.5 0.7 reduce.9
  49.2 0.1 squeeze.2
  49.2 0.1 copy.23
  49.3 0.1 convert_reduce_fusion
  49.4 0.2 add_reduce_fusion
  49.6 0.2 select_reduce_fusion
  49.8 5.9 %scatter_custom_fusion = bf16[64,36864]{1,0:T(8,128)(2,1)} fusion(s32[16]{0:T(128)S(1)} %get-tuple-element.16, bf16[16,36864]{1,0:T(8,128)(2,1)} %param.6, bf16[]{:T(256)} %constant.87.clone.1), kind=kCustom, calls=%fused_computation.11 | custom fusion | bytes 4719104 | tf_op jit(solution)/shard_map/scatter | solution.py:45
  55.7 7.3 %reduce.11 = bf16[64,36864]{1,0:T(8,128)(2,1)} reduce(bf16[64,1,36864]{2,0,1:T(8,128)(2,1)} %bitcast.114, bf16[]{:T(256)} %broadcast.561), dimensions={1}, to_apply=%copy.27.reduce_sub_computation | reduce | bytes 9437186 | tf_op jit(solution)/shard_map/reshape | solution.py:45
  63.0 8.3 %reshape.482 = bf16[64,2,18432]{2,1,0:T(2,128)(2,1)} reshape(bf16[64,36864]{1,0:T(8,128)(2,1)} %reduce.11) | data formatting | bytes 9437184
  71.3 183.3 %all-to-all-done = bf16[64,2,18432]{2,1,0:T(2,128)(2,1)} async-done(((bf16[64,2,18432]{2,1,0:T(2,128)(2,1)}), bf16[64,2,18432]{2,1,0:T(2,128)(2,1)}, u32[]{:S(2)}, u32[]{:S(2)}) %all-to-all-start) | async-done | bytes 4718624 | tf_op jit(solution)/shard_map/all_to_all | solution.py:67
  254.6 11.8 %all-to-all-start.1 = ((bf16[64,2,18432]{2,1,0:T(2,128)(2,1)}), bf16[64,2,18432]{2,1,0:T(2,128)(2,1)}, u32[]{:S(2)}, u32[]{:S(2)}) async-start(bf16[64,2,18432]{2,1,0:T(2,128)(2,1)} %reshape.482), calls=%async_computation.1 | async-start | bytes 9437184 | tf_op jit(solution)/shard_map/all_to_all | solution.py:47
  266.4 0.1 copy.28
  266.5 0.0 copy-done.3
  266.5 0.1 fusion.30
  266.6 0.7 gather_fusion
  267.4 0.2 gather.33
  267.6 0.1 reshape.380
  267.7 0.0 copy-done.4
  267.7 0.1 reshape.422
  267.8 0.6 gather_fusion.3
  268.4 0.1 fusion.33
  268.5 20.2 %reshape.481 = bf16[64,1,36864]{2,1,0:T(2,128)(2,1)} reshape(bf16[64,2,18432]{2,1,0:T(2,128)(2,1)} %all-to-all-done) | data formatting | bytes 9437184
  288.7 11.0 %copy.22 = bf16[64,1,36864]{2,0,1:T(8,128)(2,1)} copy(bf16[64,1,36864]{2,1,0:T(2,128)(2,1)} %reshape.481) | data formatting | bytes 9437184 | tf_op jit(solution)/shard_map/all_to_all | solution.py:67
  299.8 2.2 gather_fusion.2
  302.0 0.2 gather.37
  302.2 0.1 broadcast_select_fusion
  302.3 0.9 fusion.36
  303.2 3.0 collective-permute-start.1
  306.2 3.4 collective-permute-start
  309.6 163.1 %all-to-all-done.1 = bf16[64,2,18432]{2,1,0:T(2,128)(2,1)} async-done(((bf16[64,2,18432]{2,1,0:T(2,128)(2,1)}), bf16[64,2,18432]{2,1,0:T(2,128)(2,1)}, u32[]{:S(2)}, u32[]{:S(2)}) %all-to-all-start.1) | async-done | bytes 4718624 | tf_op jit(solution)/shard_map/all_to_all | solution.py:47
  472.7 20.2 %reshape.483 = bf16[64,1,36864]{2,1,0:T(2,128)(2,1)} reshape(bf16[64,2,18432]{2,1,0:T(2,128)(2,1)} %all-to-all-done.1) | data formatting | bytes 9437184
  492.9 11.0 %copy.34 = bf16[64,1,36864]{2,0,1:T(8,128)(2,1)} copy(bf16[64,1,36864]{2,1,0:T(2,128)(2,1)} %reshape.483) | data formatting | bytes 9437184
  503.9 5.2 gather_fusion.4
  509.1 1.8 reshape.381
  511.0 0.0 collective-permute-done.1
  511.0 0.0 collective-permute-done
  511.0 0.7 gather_fusion.5
  511.8 2.3 fusion.37
  514.1 7.3 %collective-permute-start.3 = (bf16[2,192,128]{2,1,0:T(8,128)(2,1)S(1)}, bf16[2,192,128]{2,1,0:T(8,128)(2,1)S(1)}, u32[]{:S(2)}, u32[]{:S(2)}) collective-permute-start(bf16[2,192,128]{2,1,0:T(8,128)(2,1)S(1)} %get-tuple-element.11), channel_id=1, source_target_pairs={{64,0},{128,64},{192,128},{256,192},{320,256},{384,320},{448,384},... | collective-permute-start | bytes 294920 | tf_op jit(solution)/shard_map/ppermute | solution.py:20
  521.3 3.1 collective-permute-start.2
  524.5 0.4 collective-permute-done.3
  524.8 1.3 collective-permute-done.2
  526.1 0.7 gather_fusion.6
  526.8 1.6 fusion.38
  528.5 1.9 collective-permute-start.5
  530.4 4.3 collective-permute-start.4
  534.7 0.4 collective-permute-done.5
  535.1 1.3 collective-permute-done.4
  536.4 0.7 gather_fusion.7
  537.1 1.4 convolution_add_fusion
  (22 shorter events, 0.2 us)
Async XLA Ops:
  0.0 2.3 copy-start
  29.0 19.5 %copy-start.2 = (s32[1,1024]{1,0:T(1,128)S(1)}, s32[1,1024]{1,0:T(1,128)}, u32[]{:S(2)}) copy-start(s32[1,1024]{1,0:T(1,128)} %param.10) | copy-start | bytes 12292
  29.0 225.6 %all-to-all-start = ((bf16[64,2,18432]{2,1,0:T(2,128)(2,1)}), bf16[64,2,18432]{2,1,0:T(2,128)(2,1)}, u32[]{:S(2)}, u32[]{:S(2)}) async-start(bf16[64,2,18432]{2,1,0:T(2,128)(2,1)} %reshape.480), calls=%async_computation | async-start | bytes 9437184 | tf_op jit(solution)/shard_map/all_to_all | solution.py:67
  71.3 195.2 %copy-start.3 = (s32[1,128]{1,0:T(1,128)S(1)}, s32[1,128]{1,0:T(1,128)}, u32[]{:S(2)}) copy-start(s32[1,128]{1,0:T(1,128)} %param.9) | copy-start | bytes 1540
  71.3 196.4 %copy-start.4 = (s32[2,8]{1,0:T(2,128)S(1)}, s32[2,8]{1,0:T(2,128)}, u32[]{:S(2)}) copy-start(s32[2,8]{1,0:T(2,128)} %param.11) | copy-start | bytes 196
  254.6 218.1 %all-to-all-start.1 = ((bf16[64,2,18432]{2,1,0:T(2,128)(2,1)}), bf16[64,2,18432]{2,1,0:T(2,128)(2,1)}, u32[]{:S(2)}, u32[]{:S(2)}) async-start(bf16[64,2,18432]{2,1,0:T(2,128)(2,1)} %reshape.482), calls=%async_computation.1 | async-start | bytes 9437184 | tf_op jit(solution)/shard_map/all_to_all | solution.py:47
  288.7 13.6 %copy-start.1 = (bf16[2,192,128]{2,1,0:T(8,128)(2,1)S(1)}, bf16[2,192,128]{2,1,0:T(8,128)(2,1)}, u32[]{:S(2)}) copy-start(bf16[2,192,128]{2,1,0:T(8,128)(2,1)} %param.8) | copy-start | bytes 294916
  303.2 207.8 %collective-permute-start.1 = (bf16[2,192,128]{2,1,0:T(8,128)(2,1)S(1)}, bf16[2,192,128]{2,1,0:T(8,128)(2,1)S(1)}, u32[]{:S(2)}, u32[]{:S(2)}) collective-permute-start(bf16[2,192,128]{2,1,0:T(8,128)(2,1)S(1)} %get-tuple-element.9), channel_id=1, source_target_pairs={{64,0},{128,64},{192,128},{256,192},{320,256},{384,320},{448,384},... | collective-permute-start | bytes 294920 | tf_op jit(solution)/shard_map/ppermute | solution.py:20
  306.2 204.8 %collective-permute-start = (bf16[2,192,128]{2,1,0:T(8,128)(2,1)S(1)}, bf16[2,192,128]{2,1,0:T(8,128)(2,1)S(1)}, u32[]{:S(2)}, u32[]{:S(2)}) collective-permute-start(bf16[2,192,128]{2,1,0:T(8,128)(2,1)S(1)} %get-tuple-element.9), channel_id=1, source_target_pairs={{0,64},{64,128},{128,192},{192,256},{256,320},{320,384},{384,448},... | collective-permute-start | bytes 294920 | tf_op jit(solution)/shard_map/ppermute | solution.py:18
  514.1 10.8 %collective-permute-start.3 = (bf16[2,192,128]{2,1,0:T(8,128)(2,1)S(1)}, bf16[2,192,128]{2,1,0:T(8,128)(2,1)S(1)}, u32[]{:S(2)}, u32[]{:S(2)}) collective-permute-start(bf16[2,192,128]{2,1,0:T(8,128)(2,1)S(1)} %get-tuple-element.11), channel_id=1, source_target_pairs={{64,0},{128,64},{192,128},{256,192},{320,256},{384,320},{448,384},... | collective-permute-start | bytes 294920 | tf_op jit(solution)/shard_map/ppermute | solution.py:20
  521.3 4.7 collective-permute-start.2
  528.5 6.6 %collective-permute-start.5 = (bf16[2,192,128]{2,1,0:T(8,128)(2,1)S(1)}, bf16[2,192,128]{2,1,0:T(8,128)(2,1)S(1)}, u32[]{:S(2)}, u32[]{:S(2)}) collective-permute-start(bf16[2,192,128]{2,1,0:T(8,128)(2,1)S(1)} %get-tuple-element.13), channel_id=1, source_target_pairs={{64,0},{128,64},{192,128},{256,192},{320,256},{384,320},{448,384},... | collective-permute-start | bytes 294920 | tf_op jit(solution)/shard_map/ppermute | solution.py:20
  530.4 5.9 %collective-permute-start.4 = (bf16[2,192,128]{2,1,0:T(8,128)(2,1)S(1)}, bf16[2,192,128]{2,1,0:T(8,128)(2,1)S(1)}, u32[]{:S(2)}, u32[]{:S(2)}) collective-permute-start(bf16[2,192,128]{2,1,0:T(8,128)(2,1)S(1)} %get-tuple-element.13), channel_id=1, source_target_pairs={{0,64},{64,128},{128,192},{192,256},{256,320},{320,384},{384,448},... | collective-permute-start | bytes 294920 | tf_op jit(solution)/shard_map/ppermute | solution.py:18
where the time goes:
time: 541 us; the launch traced here: 538 us
  waiting for transfers between devices  350 us (65%)
  local copies, waits for them, and re-layouts  105 us (19%)
  starting transfers between devices  54.3 us (10%)
  other arithmetic  22.7 us (4%)
  matrix products  6.19 us (1%)
    all_to_all x1, waiting for transfers between devices, shards(): lax.all_to_all(payload[:, None, :], 'yz', split_axis=0, concat_axis=0, ti...  183 us
    all_to_all x1, waiting for transfers between devices, shards(): lax.all_to_all(outgoing, 'yz', split_axis=0, concat_axis=0, tiled=True)  163 us
    unnamed x16, local copies, waits for them, and re-layouts  68.5 us
    all_to_all x1, starting transfers between devices, shards(): lax.all_to_all(payload[:, None, :], 'yz', split_axis=0, concat_axis=0, ti...  19.5 us
    ppermute x3, starting transfers between devices, with_halo(): lax.ppermute(head, axis, [((i + 1) % count, i) for i in range(ends)])  12.2 us
    select_n x2, other arithmetic, shards(): jnp.where(jnp.any(leaving, axis=1)[:, None], inv_factor[local_slot], jnp....  12.1 us
    all_to_all x1, starting transfers between devices, shards(): lax.all_to_all(outgoing, 'yz', split_axis=0, concat_axis=0, tiled=True)  11.8 us
    all_to_all x1, local copies, waits for them, and re-layouts, shards(): lax.all_to_all(payload[:, None, :], 'yz', split_axis=0, concat_axis=0, ti...  11 us
  transfers between devices with their start and end apart: 8, of which 6 were waited for; matrix products, arithmetic and copies ran while one was open for 18% of the time, Pallas kernels for 0%

commit v1 on v0

v1 whole, which is shorter than its diff:
```python
import functools

import jax
import jax.numpy as jnp
from jax import lax
from jax.experimental import pallas as pl
from jax.experimental.pallas import tpu as pltpu
from jax.sharding import PartitionSpec as P

MESH = pl.DeviceIdType.MESH
ITERS = 3
NX, NZ = 4, 16
NO = NX * NZ
T = 16
RB = 2
NK = 8
BS = 192
ROWS = BS * BS // 128
HALF = ROWS // 2
TRI = BS // 2
LANES = 4
PADX = 64
VMEM_LIMIT = 64_000_000


def prep_kernel(R, tmap, mig, elem, inv, route, cls, tiles, own, moved, wide, wide2, sz, srt, cnt, dist, off):
    my = lax.axis_index("yz")
    z = lax.rem(my, NZ)

    @pl.loop(0, TRI)
    def _(j):
        for k in range(3):
            at = pl.ds(pl.multiple_of((3 * j + k) * 128, 128), 128)
            wide[pl.ds(k * TRI + j, T, stride=ROWS), :] = elem[:, at].astype(jnp.float32)
            wide2[pl.ds(k * TRI + j, RB, stride=ROWS), :] = inv[:, at].astype(jnp.float32)

    @pl.loop(0, T)
    def _(t):
        tiles[t] = wide[pl.ds(pl.multiple_of(t * ROWS, ROWS), ROWS), :].astype(jnp.bfloat16)

    for b in range(RB):
        own[b] = wide2[pl.ds(b * ROWS, ROWS), :].astype(jnp.bfloat16)

    for n, bit in enumerate((NO // 2, 1)):
        q = jnp.bitwise_xor(my, bit)
        b = jnp.int32(0)
        for r in range(RB):
            src = mig[0, q * RB + r]
            b = jnp.where(src // RB == my, lax.rem(src, RB), b)
        moved[n] = own[b]
    for r in range(RB):
        src = mig[0, my * RB + r]
        home = src // RB
        cls[6, r] = jnp.where(
            home == my, lax.rem(src, RB), jnp.where(home == jnp.bitwise_xor(my, NO // 2), 2, 3)
        )

    @pl.loop(0, NZ)
    def _(v):
        cnt[v] = 0

    @pl.loop(0, T)
    def _(t):
        s = tmap[0, t] // T
        along = lax.rem(s, NZ)
        sz[t] = along
        cnt[along] = cnt[along] + 1
        across = s // NZ
        cls[0, t] = lax.rem(across + jnp.where(z + along >= NZ, 1, 0), NX)
        cls[1, t] = lax.rem(across + jnp.where(z < along, 1, 0), NX)
        a = lax.rem(my - s + NO, NO)
        cls[5, lax.rem(tmap[0, a * T + t], T)] = t

    def prefix(v, run):
        n = cnt[v]
        cnt[v] = run
        return run + n

    lax.fori_loop(0, NZ, prefix, jnp.int32(0))

    def place(t, far):
        v = sz[t]
        srt[cnt[v]] = t
        cnt[v] = cnt[v] + 1
        return far + NZ - v

    far = lax.fori_loop(0, T, place, jnp.int32(0))

    def split(i, c):
        up, down, best, m = c
        v = sz[srt[i]]
        up, down = up + v, down - (NZ - v)
        worst = jnp.maximum(up, down)
        better = worst < best
        return up, down, jnp.where(better, worst, best), jnp.where(better, i + 1, m)

    zero = jnp.int32(0)
    m = lax.fori_loop(0, T, split, (zero, far, far, zero))[3]

    @pl.loop(0, 2 * LANES * R)
    def _(p):
        route[0, p] = 0
        route[1, p] = 0
        route[2, p] = 0

    def plan(i, ends):
        up, down = ends
        t = srt[i]
        v = sz[t]
        goes_up = i < m
        d = jnp.where(goes_up, v, NZ - v)
        base = jnp.where(goes_up, 0, LANES * R)
        c = jnp.where(goes_up, up, down)
        last = c + d - 1
        lane0, lane1 = c // R, last // R

        @pl.when(d == 0)
        def _():
            cls[2, t] = 0
            cls[3, t] = 1

        @pl.when(d > 0)
        def _():
            cls[3, t] = 0

            @pl.when(lane0 == lane1)
            def _():
                route[0, base + c] = 1
                route[1, base + c] = t
                cls[2, t] = base + last

            @pl.when(lane0 != lane1)
            def _():
                route[0, base + lane1 * R] = 1
                route[1, base + lane1 * R] = t
                route[0, base + c] = 2
                route[2, base + last] = 1
                cls[2, t] = base + lane1 * R - 1

        return up + jnp.where(goes_up, d, 0), down + jnp.where(goes_up, 0, d)

    lax.fori_loop(0, T, plan, (zero, zero))


def main_kernel(
    R, route, cls, col, tiles, own, moved, rhs, out,
    recv1, recv2, send1, send2, save, xp1, xm1, xf1, xp2, xm2, xf2, init2, stage, rowt,
    got, fac, pad0, pad1, pad2, vec, mix, it,
    zr1, zr2, zs1, zs2, xr1, xr2, xs1, xs2, mr, ms, hr, hs,
):
    g = lax.axis_index("gx")
    slabs = lax.axis_size("gx")
    my = lax.axis_index("yz")
    x, z = my // NZ, lax.rem(my, NZ)
    line = x * NZ
    z_to = ({"yz": line + lax.rem(z + 1, NZ)}, {"yz": line + lax.rem(z + NZ - 1, NZ)})
    x_to = ({"yz": lax.rem(x + 1, NX) * NZ + z}, {"yz": lax.rem(x + NX - 1, NX) * NZ + z})
    m_to = ({"yz": lax.rem(x + NX // 2, NX) * NZ + z}, {"yz": my + 1 - 2 * lax.rem(my, 2)})
    g_to = ({"gx": lax.rem(g + 1, slabs)}, {"gx": lax.rem(g + slabs - 1, slabs)})
    pads = (pad0, pad1, pad2)

    def remote(src, dst, send, recv, to):
        return pltpu.make_async_remote_copy(
            src_ref=src, dst_ref=dst, send_sem=send, recv_sem=recv, device_id=to, device_id_type=MESH
        )

    barrier = pltpu.get_barrier_semaphore()
    greet = (*z_to, *x_to, m_to[0], *g_to)
    for to in greet:
        pl.semaphore_signal(barrier, inc=1, device_id=to, device_id_type=MESH)
    pl.semaphore_wait(barrier, len(greet))

    def moves():
        return [remote(moved.at[n], got.at[n], ms.at[n], mr.at[n], m_to[n]) for n in range(2)]

    for c in moves():
        c.start()

    for buf in (*pads, vec):
        n = buf.shape[0]
        buf[:, 0:PADX, :] = jnp.zeros((n, PADX, 128), jnp.bfloat16)
        buf[:, PADX + BS:, :] = jnp.zeros((n, PADX, 128), jnp.bfloat16)
    save[...] = jnp.zeros_like(save)

    lanes = [(d, j) for j in reversed(range(LANES)) for d in range(2)]

    def z_copy(recv, sendb, zr, zs, d, j, r):
        p = (d * LANES + j) * R + r
        k = (d * LANES + j) * 2 + lax.rem(r, 2)
        return remote(sendb.at[k], recv.at[p], zs.at[k], zr.at[p], z_to[d])

    def x_first(src, xp, xm, xr, xs, t, d):
        return remote(src.at[t], (xp, xm)[d].at[t], xs.at[d * T + t], xr.at[d * T + t], x_to[d])

    def x_second(xp, xm, xf, xr, xs, t, odd):
        src = (xm if odd else xp).at[t]
        return remote(src, xf.at[t], xs.at[2 * T + t], xr.at[2 * T + t], x_to[1 if odd else 0])

    def phase(first, x_src, recv, sendb, zr, zs, xp, xm, xf, xr, xs, between):
        pend = None
        for d, j in lanes:
            k = (d * LANES + j) * 2
            sendb[k] = first(route[1, (d * LANES + j) * R])
            if pend is not None:
                pend.start()
            pend = z_copy(recv, sendb, zr, zs, d, j, 0)
        pend.start()

        @pl.loop(0, T)
        def _(t):
            for d in range(2):
                x_first(x_src, xp, xm, xr, xs, t, d).start()

        if between is not None:
            between()

        @pl.loop(1, R)
        def _(r):
            pend = None
            for d, j in lanes:
                p = (d * LANES + j) * R + r
                z_copy(recv, sendb, zr, zs, d, j, r - 1).wait_recv()
                come = recv[p - 1]
                if j > 0:
                    s = d * LANES + j
                    save[s] = lax.select(route[2, p - 1] == 1, come, save[s])
                mode = route[0, p]
                new = first(route[1, p])
                if j < LANES - 1:
                    new = lax.select(mode == 2, save[d * LANES + j + 1], new)
                new = lax.select(mode == 0, come, new)

                @pl.when(r >= 2)
                def _():
                    z_copy(recv, sendb, zr, zs, d, j, r - 2).wait_send()

                sendb[(d * LANES + j) * 2 + lax.rem(r, 2)] = new
                if pend is not None:
                    pend.start()
                pend = z_copy(recv, sendb, zr, zs, d, j, r)
            pend.start()

            @pl.when(r <= T // 2)
            def _():
                t = 2 * (r - 1)
                x_first(x_src, xp, xm, xr, xs, t, 0).wait_recv()
                x_second(xp, xm, xf, xr, xs, t, False).start()
                x_first(x_src, xp, xm, xr, xs, t + 1, 1).wait_recv()
                x_second(xp, xm, xf, xr, xs, t + 1, True).start()

        @pl.loop(0, T // 2)
        def _(h):
            t = 2 * h
            x_first(x_src, xp, xm, xr, xs, t, 0).wait_send()
            x_first(x_src, xp, xm, xr, xs, t, 1).wait()
            x_first(x_src, xp, xm, xr, xs, t + 1, 0).wait()
            x_first(x_src, xp, xm, xr, xs, t + 1, 1).wait_send()
            for c in (x_second(xp, xm, xf, xr, xs, t, False), x_second(xp, xm, xf, xr, xs, t + 1, True)):
                c.wait()

        for d, j in lanes:
            last = z_copy(recv, sendb, zr, zs, d, j, R - 1)
            last.wait()
            z_copy(recv, sendb, zr, zs, d, j, R - 2).wait_send()

    def of_four(n, a, b, c, d):
        return lax.select(n == 0, a, lax.select(n == 1, b, lax.select(n == 2, c, d)))

    phase(
        lambda t: tiles[t, HALF:, :], tiles.at[:, 0:HALF, :], recv1, send1, zr1, zs1,
        xp1, xm1, xf1, xr1, xs1, None,
    )

    @pl.loop(0, T)
    def _(t):
        stage[t] = lax.select(cls[3, t] == 1, tiles[t, HALF:, :], recv1[cls[2, t]])
        init2[t] = of_four(cls[0, t], tiles[t, 0:HALF, :], xp1[t], xf1[t], xm1[t])

    def product(m, v):
        f0, f1, f2 = m[0:TRI], m[TRI:2 * TRI], m[2 * TRI:]
        even = jnp.dot(
            jnp.concatenate([f0, f1], axis=1), v[PADX:, :], preferred_element_type=jnp.float32
        )
        odd = jnp.dot(
            jnp.concatenate([f1, f2], axis=1), v[:PADX + BS, :], preferred_element_type=jnp.float32
        )
        return even, odd

    def halo(s):
        b = pads[s]
        mine = b.at[RB:2 * RB, PADX:PADX + BS, :]
        return (
            remote(mine, b.at[0:RB, PADX:PADX + BS, :], hs.at[2 * s], hr.at[2 * s], g_to[0]),
            remote(mine, b.at[2 * RB:, PADX:PADX + BS, :], hs.at[2 * s + 1], hr.at[2 * s + 1], g_to[1]),
        )

    def spread(ref, r, even, odd):
        ref[pl.ds(r * BS, TRI, stride=2), :] = even
        ref[pl.ds(r * BS + 1, TRI, stride=2), :] = odd

    def begin():
        for c in moves():
            c.wait()
        for r in range(RB):
            fac[r] = of_four(cls[6, r], own[0], own[1], got[0], got[1])
            vec[r, PADX:PADX + BS, :] = rhs[r]
        for r in range(RB):
            even, odd = product(fac[r], vec[r])
            spread(it, r, even, odd)
        for r in range(RB):
            pads[0][RB + r, PADX:PADX + BS, :] = it[pl.ds(r * BS, BS), :].astype(jnp.bfloat16)
        for c in halo(0):
            c.start()

    phase(
        lambda t: init2[t], stage, recv2, send2, zr2, zs2, xp2, xm2, xf2, xr2, xs2, begin,
    )

    @pl.loop(0, T)
    def _(p):
        t = cls[5, p]
        rowt[p, 0:HALF, :] = lax.select(cls[3, t] == 1, init2[t], recv2[cls[2, t]])
        rowt[p, HALF:, :] = of_four(cls[1, t], stage[t], xp2[t], xf2[t], xm2[t])

    for s in range(ITERS):
        b = pads[s]
        for c in halo(s):
            c.wait()

        @pl.when(g == 0)
        def _():
            b[0:RB, PADX:PADX + BS, :] = jnp.zeros((RB, BS, 128), jnp.bfloat16)

        @pl.when(g == slabs - 1)
        def _():
            b[2 * RB:, PADX:PADX + BS, :] = jnp.zeros((RB, BS, 128), jnp.bfloat16)

        for r in range(RB):
            even = odd = jnp.zeros((TRI, 128), jnp.float32)
            for k in range(NK):
                e, o = product(rowt[r * NK + k], b[col[r, k]])
                even, odd = even + e, odd + o
            spread(mix, r, even, odd)
        for r in range(RB):
            rounded = b[RB + r, PADX:PADX + BS, :].astype(jnp.float32)
            applied = rounded + mix[pl.ds(r * BS, BS), :]
            vec[r, PADX:PADX + BS, :] = (rhs[r].astype(jnp.float32) - applied).astype(jnp.bfloat16)
        for r in range(RB):
            even, odd = product(fac[r], vec[r])
            spread(mix, r, even, odd)
        if s < ITERS - 1:
            for r in range(RB):
                new = it[pl.ds(r * BS, BS), :] + mix[pl.ds(r * BS, BS), :]
                it[pl.ds(r * BS, BS), :] = new
                pads[s + 1][RB + r, PADX:PADX + BS, :] = new.astype(jnp.bfloat16)
            for c in halo(s + 1):
                c.start()
        else:
            for r in range(RB):
                out[r] = it[pl.ds(r * BS, BS), :] + mix[pl.ds(r * BS, BS), :]


def shards(elem_tiles, inv_factor, rhs, mig_source, tile_target, col_index):
    R = 16
    n_pos = 2 * LANES * R
    smem = pl.BlockSpec(memory_space=pltpu.SMEM)
    vmem = pl.BlockSpec(memory_space=pltpu.VMEM)
    bf, f32, i32 = jnp.bfloat16, jnp.float32, jnp.int32
    route, cls, tiles, own, moved = pl.pallas_call(
        functools.partial(prep_kernel, R),
        name="prep",
        out_shape=(
            jax.ShapeDtypeStruct((3, n_pos), i32),
            jax.ShapeDtypeStruct((7, T), i32),
            jax.ShapeDtypeStruct((T, ROWS, 128), bf),
            jax.ShapeDtypeStruct((RB, ROWS, 128), bf),
            jax.ShapeDtypeStruct((2, ROWS, 128), bf),
        ),
        in_specs=[smem, smem, vmem, vmem],
        out_specs=(smem, smem, vmem, vmem, vmem),
        scratch_shapes=[
            pltpu.VMEM((T * ROWS, 128), f32),
            pltpu.VMEM((RB * ROWS, 128), f32),
            pltpu.SMEM((T,), i32),
            pltpu.SMEM((T,), i32),
            pltpu.SMEM((NZ,), i32),
            pltpu.SMEM((T,), i32),
            pltpu.SMEM((T,), i32),
        ],
        compiler_params=pltpu.CompilerParams(vmem_limit_bytes=VMEM_LIMIT),
    )(tile_target, mig_source, elem_tiles, inv_factor)

    half = lambda n: pltpu.VMEM((n, HALF, 128), bf)
    padded = lambda n: pltpu.VMEM((n, 2 * PADX + BS, 128), bf)
    dma = pltpu.SemaphoreType.DMA
    return pl.pallas_call(
        functools.partial(main_kernel, R),
        name="main",
        out_shape=jax.ShapeDtypeStruct((RB, BS, 128), f32),
        in_specs=[smem, smem, smem, vmem, vmem, vmem, vmem],
        out_specs=vmem,
        scratch_shapes=[
            half(n_pos), half(n_pos), half(4 * LANES), half(4 * LANES), half(2 * LANES),
            half(T), half(T), half(T), half(T), half(T), half(T), half(T), half(T),
            pltpu.VMEM((T, ROWS, 128), bf),
            pltpu.VMEM((2, ROWS, 128), bf),
            pltpu.VMEM((RB, ROWS, 128), bf),
            padded(3 * RB), padded(3 * RB), padded(3 * RB), padded(RB),
            pltpu.VMEM((RB * BS, 128), f32),
            pltpu.VMEM((RB * BS, 128), f32),
            dma((n_pos,)), dma((n_pos,)), dma((4 * LANES,)), dma((4 * LANES,)),
            dma((3 * T,)), dma((3 * T,)), dma((3 * T,)), dma((3 * T,)),
            dma((2,)), dma((2,)), dma((2 * ITERS,)), dma((2 * ITERS,)),
        ],
        compiler_params=pltpu.CompilerParams(
            collective_id=0, has_side_effects=True, vmem_limit_bytes=VMEM_LIMIT
        ),
    )(route, cls, col_index, tiles, own, moved, rhs)


def solution(mesh):
    placed = (
        P(("gx", "yz"), None),
        P(("gx", "yz"), None),
        P(("gx", "yz"), None, None),
        P("gx", None),
        P("gx", None),
        P(("gx", "yz"), None),
    )
    return jax.shard_map(
        shards, mesh=mesh, in_specs=placed, out_specs=P(("gx", "yz"), None, None), check_vma=False
    )
```

time: 541 us -> 176 us (0.33)
  waiting for transfers between devices: 350 us -> 0 us
  Pallas kernels: 0 us -> 174 us
  local copies, waits for them, and re-layouts: 105 us -> 1.62 us
  starting transfers between devices: 54.3 us -> 0 us
  other arithmetic: 22.7 us -> 0 us
  matrix products: 6.19 us -> 0 us
    all_to_all x2 -> x0, waiting for transfers between devices: 346 us -> none  [the longest x1 183 us: shards(): lax.all_to_all(payload[:, None, :], 'yz', split_axis=0, concat_axis=0, ti...]
    pallas_call x0 -> x2, Pallas kernels: none -> 174 us  [the longest x1 166 us: shards(): pl.pallas_call(functools.partial(main_kernel, R), name='main', out_shape=...]
    unnamed x16 -> x1, local copies, waits for them, and re-layouts: 68.5 us -> 1.62 us
    all_to_all x2 -> x0, starting transfers between devices: 31.3 us -> none  [the longest x1 19.5 us: shards(): lax.all_to_all(payload[:, None, :], 'yz', split_axis=0, concat_axis=0, ti...]
    ppermute x6 -> x0, starting transfers between devices: 23 us -> none  [the longest x3 12.2 us: with_halo(): lax.ppermute(head, axis, [((i + 1) % count, i) for i in range(ends)])]
    gather x10 -> x0, local copies, waits for them, and re-layouts: 17.1 us -> none  [the longest x1 5.74 us: shards(): inv_factor[local_slot]]
    select_n x9 -> x0, other arithmetic: 12.3 us -> none  [the longest x2 12.1 us: shards(): jnp.where(jnp.any(leaving, axis=1)[:, None], inv_factor[local_slot], jnp....]
    all_to_all x1 -> x0, local copies, waits for them, and re-layouts: 11 us -> none  [shards(): lax.all_to_all(payload[:, None, :], 'yz', split_axis=0, concat_axis=0, ti...]
  transfers between devices with their start and end apart: 8 -> 0, of which waited for: 6 -> 0; matrix products, arithmetic and copies ran while one was open for 18% -> 0% of each run, Pallas kernels for 0% -> 0%
where the time goes in v1:
time: 176 us; the launch traced here: 175 us
  Pallas kernels  174 us (99%)
    pallas_call x1, Pallas kernels, shards(): pl.pallas_call(functools.partial(main_kernel, R), name='main', out_shape=...  166 us
    pallas_call x1, Pallas kernels, shards(): pl.pallas_call(functools.partial(prep_kernel, R), name='prep', out_shape=...  7.99 us

profile of v1, /device:TPU:1, one launch (start us, length us, event | category | flops | bytes accessed | tf_op | source)
XLA Modules:
  0.0 175.4 jit_solution(17412910135609894511)
XLA Ops:
  0.0 8.0 %prep.1 = (s32[3,128]{1,0:T(4,128)}, s32[7,16]{1,0:T(8,128)}, bf16[16,288,128]{2,1,0:T(8,128)(2,1)}, bf16[2,288,128]{2,1,0:T(8,128)(2,1)}, bf16[2,288,128]{2,1,0:T(8,128)(2,1)}) custom-call(s32[1,1024]{1,0:T(1,128)} %tmap.1, s32[1,128]{1,0:T(1,128)} %mig.1, bf16[16,36864]{1,0:T(8,128)(2,1)} %elem.1, bf16[2,36864]{1,0:T(2,128)(2,1)} %inv.1), custom_call_target="tpu_custom_call" | custom-call | tf_op jit(solution)/shard_map/prep/pallas_call | solution.py:369
  8.0 165.7 %main.1 = f32[2,192,128]{2,1,0:T(8,128)} custom-call(s32[3,128]{1,0:T(4,128)} %get-tuple-element.10.route, s32[7,16]{1,0:T(8,128)} %get-tuple-element.11.cls, s32[2,8]{1,0:T(2,128)} %col.1, bf16[16,288,128]{2,1,0:T(8,128)(2,1)} %get-tuple-element.12.tiles, bf16[2,288,128]{2,1,0:T(8,128)(2,1)} %get-tuple-element.13.own, ...), custom_call_target="tpu_custom_call" | custom-call | tf_op jit(solution)/shard_map/main/pallas_call | solution.py:396
  173.7 1.6 copy.8
